TPU v7x, 128 devices: a whole 4x4x4 slice. The times are simulated.
128 devices in a mesh: hi: 16 (over y, x), lo: 8 (over z, core).
Axes of the slice: x: 4, y: 4, z: 4, core: 2. Of those that a mesh axis runs over, the one named last changes fastest.
Arguments:
- previous: float32 [32, 2097152], P(None, ('hi', 'lo')), may hold values from -6 to 6
- current: float32 [32, 2097152], P(None, ('hi', 'lo')), may hold values from -6 to 6
- field_levels: int32 [21], replicated, may hold values from -4 to 4
- bond_levels: int32 [20], replicated, may hold values from 1 to 3
Outputs:
- ortho_block: float32 [32, 2097152], P(None, ('hi', 'lo'))
- upper_factor: float32 [32, 32], replicated
All inputs are finite; a program needn't handle non-finite values.
Results may differ from a plain program's by a relative error of at most 0.00005.
Values sent between devices are 32-bit elements; how exact they have to be, the bound alone decides.
A program may use at most 64 MiB of HBM per device.

v0:
```python
import jax
import jax.numpy as jnp
from jax import lax
from jax.sharding import PartitionSpec as P

FIELD_STEP = 0.75
COUPLING_STEP = 0.5


def chain_matrix(couplings, bit_count, bond_list):
    width = 2**bit_count
    rows = lax.iota(jnp.int32, width)[:, None]
    cols = lax.iota(jnp.int32, width)[None, :]
    matrix = jnp.zeros((width, width), jnp.float32)
    for site_number, spot in bond_list:
        differ = cols >> spot & 1 != cols >> spot + 1 & 1
        target = rows == cols ^ 3 << spot
        matrix = matrix + jnp.where(differ & target, 0.5 * couplings[site_number], 0.0)
    return matrix


def cross_flip(values, coupling, low_spot):
    width = values.shape[-1]
    index = lax.iota(jnp.int32, width)
    permute = (index[:, None] == index[None, :] ^ 1 << low_spot).astype(jnp.float32)
    moved = jnp.einsum("vatbl,lj->vatbj", values, permute, precision=lax.Precision.HIGHEST)
    flipped = jnp.flip(moved, axis=2)
    upper = lax.iota(jnp.int32, 2)[:, None]
    keep = (index[None, :] >> low_spot & 1 != upper).astype(jnp.float32)
    return 0.5 * coupling * flipped * keep[None, None, :, None, :]


def local(previous, current, field_levels, bond_levels):
    vectors, amp_count = current.shape
    site_count = field_levels.shape[0]
    devices = lax.axis_size("hi") * lax.axis_size("lo")
    local_bits = amp_count.bit_length() - 1
    global_bits = devices.bit_length() - 1
    rest_bits = local_bits - global_bits
    device = lax.axis_index("hi") * lax.axis_size("lo") + lax.axis_index("lo")
    local_index = lax.iota(jnp.int32, amp_count)
    top_width = 2**global_bits
    low_width = 2**rest_bits

    def position(site_number):
        if site_number < global_bits:
            return rest_bits + site_number
        return site_number - global_bits

    def spin_value(site_number):
        if site_number < local_bits:
            return 0.5 - (local_index >> position(site_number) & 1).astype(jnp.float32)
        return 0.5 - (device >> site_number - local_bits & 1).astype(jnp.float32)

    fields = FIELD_STEP * field_levels.astype(jnp.float32)
    couplings = COUPLING_STEP * bond_levels.astype(jnp.float32)
    diagonal = jnp.zeros((amp_count,), jnp.float32)
    for site_number in range(site_count):
        diagonal = diagonal + fields[site_number] * spin_value(site_number)
        if site_number < site_count - 1:
            diagonal = diagonal + couplings[site_number] * spin_value(site_number) * spin_value(
                site_number + 1
            )
    top_matrix = chain_matrix(
        couplings,
        global_bits,
        [(site_number, site_number) for site_number in range(global_bits - 1)],
    )
    low_matrix = chain_matrix(
        couplings,
        rest_bits,
        [
            (site_number, site_number - global_bits)
            for site_number in range(global_bits, local_bits - 1)
        ],
    )
    blocks = current.reshape(vectors, top_width, low_width)
    applied = diagonal[None, :] * current
    applied = applied + jnp.einsum(
        "vtl,tu->vul", blocks, top_matrix, precision=lax.Precision.HIGHEST
    ).reshape(vectors, amp_count)
    applied = applied + jnp.einsum(
        "vtl,lu->vtu", blocks, low_matrix, precision=lax.Precision.HIGHEST
    ).reshape(vectors, amp_count)
    joined = cross_flip(
        current.reshape(vectors, 1, 2, top_width // 2, low_width), couplings[global_bits - 1], 0
    )
    applied = applied + joined.reshape(vectors, amp_count)
    far_matrix = chain_matrix(
        couplings,
        global_bits,
        [
            (site_number, site_number - local_bits)
            for site_number in range(local_bits, site_count - 1)
        ],
    )
    shaped = current.reshape(vectors, devices, amp_count // devices)
    arrived = lax.all_to_all(shaped, ("hi", "lo"), split_axis=1, concat_axis=1, tiled=True)
    count = arrived.shape[0]
    bond_terms = jnp.einsum(
        "vtl,tu->vul", arrived, far_matrix, precision=lax.Precision.HIGHEST
    ).reshape(count, amp_count)
    seam = cross_flip(
        arrived.reshape(count, top_width // 2, 2, 1, low_width),
        couplings[local_bits - 1],
        rest_bits - 1,
    )
    bond_terms = bond_terms + seam.reshape(count, amp_count)
    remote_part = lax.all_to_all(
        bond_terms.reshape(arrived.shape), ("hi", "lo"), split_axis=1, concat_axis=1, tiled=True
    ).reshape(vectors, amp_count)
    filtered = 4.0 / site_count * (applied + remote_part) - previous
    local_gram = jnp.dot(filtered, filtered.T, precision=lax.Precision.HIGHEST) / (
        amp_count * devices
    )
    gram_matrix = lax.psum(local_gram, ("hi", "lo"))
    lower_factor = jnp.linalg.cholesky(gram_matrix)
    inverse = jax.scipy.linalg.solve_triangular(
        lower_factor, jnp.eye(vectors, dtype=jnp.float32), lower=True
    )
    ortho_block = jnp.dot(inverse, filtered, precision=lax.Precision.HIGHEST)
    return (ortho_block, lower_factor.T)


def solution(mesh):
    in_specs = (P(None, ("hi", "lo")), P(None, ("hi", "lo")), P(), P())
    out_specs = (P(None, ("hi", "lo")), P())
    return jax.shard_map(local, mesh=mesh, in_specs=in_specs, out_specs=out_specs, check_vma=False)
```

profile of v0, /device:TPU:1, one launch (start us, length us, event | category | flops | bytes accessed | tf_op | source)
XLA Modules:
  0.0 200.1 jit_solution(15617030087911046846)
XLA Ops:
  0.6 3.2 %copy_bitcast_fusion = f32[32,128,128]{2,0,1:T(8,128)} fusion(f32[32,16384]{1,0:T(8,128)} %param.5), kind=kLoop, calls=%fused_computation.6 | loop fusion | bytes 4194304 | tf_op jit(solution)/shard_map/reshape | solution.py:77
  3.8 0.0 copy-start
  3.8 0.0 copy-start.1
  3.8 11.5 %all-to-all-start = ((f32[32,128,128]{2,0,1:T(8,128)}), f32[32,128,128]{2,0,1:T(8,128)S(1)}, u32[]{:S(2)}, u32[]{:S(2)}) async-start(f32[32,128,128]{2,0,1:T(8,128)} %copy_bitcast_fusion), calls=%async_computation | async-start | bytes 4194304 | tf_op jit(solution)/shard_map/all_to_all | solution.py:98
  15.3 0.0 copy-done
  15.4 0.7 fusion.153
  20.4 0.0 copy-done.1
  20.4 25.0 %all-to-all-done = f32[32,128,128]{2,0,1:T(8,128)S(1)} async-done(((f32[32,128,128]{2,0,1:T(8,128)}), f32[32,128,128]{2,0,1:T(8,128)S(1)}, u32[]{:S(2)}, u32[]{:S(2)}) %all-to-all-start) | async-done | bytes 2097184 | tf_op jit(solution)/shard_map/all_to_all | solution.py:98
  45.4 2.3 %fusion.7 = f32[32,64,2,128]{3,1,2,0:T(8,128)S(1)} fusion(f32[32,64,2,128]{3,0,2,1:T(8,128)S(1)} %bitcast.129, s32[128]{0:T(128)S(1)} %iota_xor_fusion), kind=kOutput, calls=%fused_computation.14 | convolution fusion | flops 805322752 | bytes 4194816 | tf_op jit(solution)/shard_map/vatbl,lj->vatbj/dot_general | solution.py:26
  47.7 0.3 multiply_multiply_fusion
  48.1 1.7 copy.31
  49.8 3.2 %bitcast_add_fusion.3 = f32[32,128,128]{2,1,0:T(8,128)S(1)} fusion(f32[32,128,128]{2,1,0:T(8,128)S(1)} %bitcast.133, f32[32,128,128]{2,0,1:T(8,128)S(1)} %all-to-all-done, f32[]{:T(128)S(6)} %mul.670, f32[]{:T(128)S(6)} %mul.669, f32[]{:T(128)S(6)} %mul.668, f32[]{:T(128)S(6)} %mul.667, f32[]{:T(128)S(6)} %mul.666, f32[]{:T(128)S(6)} %mul.665, ...), kind=kOutput, calls=%fused_computation.7 | convolution fusion | flops 806207488 | bytes 6295320 | tf_op jit(solution)/shard_map/vtl,tu->vul/dot_general | solution.py:100
  53.0 2.5 %copy.32 = f32[32,128,128]{2,0,1:T(8,128)} copy(f32[32,128,128]{2,1,0:T(8,128)S(1)} %bitcast_add_fusion.3) | data formatting | bytes 4194304 | tf_op jit(solution)/shard_map/add | solution.py:108
  55.5 5.9 %all-to-all-start.1 = ((f32[32,128,128]{2,0,1:T(8,128)}), f32[32,128,128]{2,0,1:T(8,128)}, u32[]{:S(2)}, u32[]{:S(2)}) async-start(f32[32,128,128]{2,0,1:T(8,128)} %copy.32), calls=%async_computation.1 | async-start | bytes 4194304 | tf_op jit(solution)/shard_map/all_to_all | solution.py:109
  61.4 0.7 fusion.151
  74.1 2.0 copy.42
  76.1 3.4 %convolution_bitcast_fusion.1 = f32[32,128,128]{1,2,0:T(8,128)} fusion(f32[32,128,128]{2,1,0:T(8,128)S(1)} %bitcast.125, f32[]{:T(128)S(6)} %mul.659, f32[]{:T(128)S(6)} %mul.658, f32[]{:T(128)S(6)} %mul.657, f32[]{:T(128)S(6)} %mul.656, f32[]{:T(128)S(6)} %mul.655, f32[]{:T(128)S(6)} %mul.654, s32[128]{0:T(128)S(1)} %get-tuple-element.52, ...), kind=kOutput, calls=%fused_computation.16 | convolution fusion | flops 805683200 | bytes 4198168 | tf_op jit(solution)/shard_map/vtl,lu->vtu/dot_general | solution.py:82
  79.5 2.9 %copy.27 = f32[32,128,128]{2,1,0:T(8,128)} copy(f32[32,128,128]{1,2,0:T(8,128)} %convolution_bitcast_fusion.1) | data formatting | bytes 4194304 | tf_op jit(solution)/shard_map/vtl,lu->vtu/dot_general | solution.py:82
  86.2 0.6 fusion.152
  86.7 17.3 %add_add_fusion = f32[16384]{0:T(1024)S(1)} fusion(f32[]{:T(128)S(6)} %mul.645, f32[]{:T(128)S(6)} %mul.644, f32[]{:T(128)S(6)} %mul.642, f32[]{:T(128)S(6)} %mul.641, f32[]{:T(128)S(6)} %mul.639, f32[]{:T(128)S(6)} %mul.638, f32[]{:T(128)S(6)} %mul.636, f32[]{:T(128)S(6)} %mul.635, f32[]{:T(128)S(6)} %mul.633, f32[]{:T(128)S(6)} %mul.632, f32[]{:T(128)S(6)} %mul.630, ...), kind=kLoop, calls=%fused_computation.63 | loop fusion | flops 2260992 | bytes 65704 | tf_op jit(solution)/shard_map/add | solution.py:59
  104.1 1.1 convolution_bitcast_fusion
  105.2 1.6 multiply_multiply_fusion.1
  106.8 3.4 %fusion.14 = f32[128,32,128]{2,0,1:T(8,128)} fusion(f32[32,128,128]{2,1,0:T(8,128)S(1)} %bitcast.127, f32[]{:T(128)S(6)} %mul.653, s32[128]{0:T(128)S(1)} %get-tuple-element.52, f32[]{:T(128)S(6)} %mul.652, s32[128]{0:T(128)S(1)} %get-tuple-element.53, f32[]{:T(128)S(6)} %mul.651, s32[128]{0:T(128)S(1)} %get-tuple-element.54, f32[]{:T(128)S(6)} %mul.650, ...), kind=kOutput, calls=%fused_computation.20 | convolution fusion | flops 805683200 | bytes 4198168 | tf_op jit(solution)/shard_map/vtl,tu->vul/dot_general | solution.py:79
  110.2 0.0 all-to-all-done.1
  110.2 9.6 %fusion.2 = f32[32,16384]{1,0:T(8,128)S(1)} fusion(f32[32,16384]{1,0:T(8,128)} %param.4, f32[4,8,128,128]{3,2,1,0:T(8,128)} %bitcast.130, f32[4,8,128,128]{3,2,1,0:T(8,128)} %bitcast.132, f32[4,8,128,128]{3,2,1,0:T(8,128)} %bitcast.131, f32[32,16384]{1,0:T(8,128)} %param.5, f32[16384]{0:T(1024)S(1)} %add_add_fusion, f32[32,128,128]{2,0,1:T(8,128)} %all-to-all-done.1), kind=kLoop, calls=%fused_computation.3 | loop fusion | flops 3670016 | bytes 14745600 | tf_op jit(solution)/shard_map/sub | solution.py:112
  119.8 1.8 convolution_multiply_fusion
  121.6 67.6 %psum.7 = f32[32,32]{0,1:T(8,128)S(1)} all-reduce(f32[32,32]{0,1:T(8,128)S(1)} %convolution_multiply_fusion), channel_id=1, replica_groups=mesh['hi'=16,'lo'=8] {'hi','lo'}, use_global_device_ids=true, to_apply=%region_0.1 | all-reduce | flops 1024 | bytes 8192 | tf_op jit(solution)/shard_map/psum | solution.py:116
  189.2 0.1 copy.35
  189.3 2.9 %cholesky.17 = f32[32,32]{1,0:T(8,128)S(1)} custom-call(f32[32,32]{1,0:T(8,128)S(1)} %fusion.138), custom_call_target="Cholesky" | custom-call | tf_op jit(solution)/shard_map/jit(cholesky)/cholesky | solution.py:117
  192.2 0.6 compare_reduce_fusion
  192.9 0.7 fusion.139
  193.5 2.4 %custom-call.7 = f32[1,32,32]{1,2,0:T(8,128)S(1)} custom-call(f32[1,32,32]{2,1,0:T(8,128)S(1)} %get-tuple-element.11), custom_call_target="InvertDiagBlocksLowerTriangular" | custom-call | tf_op jit(solution)/shard_map/jit(_solve_triangular)/triangular_solve | solution.py:118
  196.0 0.2 fusion.136
  196.2 3.2 %fusion.154 = f32[32,16384]{1,0:T(8,128)} fusion(f32[32,32]{1,0:T(8,128)S(1)} %fusion.136, f32[32,16384]{1,0:T(8,128)S(1)} %fusion.2), kind=kOutput, calls=%fused_computation.175 | convolution fusion | flops 201326592 | bytes 4198400 | tf_op jit(solution)/shard_map/dot_general | solution.py:121
  199.4 0.7 copy.36
  (16 shorter events, 0.1 us)
Async XLA Ops:
  3.8 11.5 %copy-start = (s32[20]{0:T(128)S(1)}, s32[20]{0:T(128)}, u32[]{:S(2)}) copy-start(s32[20]{0:T(128)} %param.7) | copy-start | bytes 244
  3.8 16.6 %copy-start.1 = (s32[21]{0:T(128)S(1)}, s32[21]{0:T(128)}, u32[]{:S(2)}) copy-start(s32[21]{0:T(128)} %param.6) | copy-start | bytes 256
  3.8 41.6 %all-to-all-start = ((f32[32,128,128]{2,0,1:T(8,128)}), f32[32,128,128]{2,0,1:T(8,128)S(1)}, u32[]{:S(2)}, u32[]{:S(2)}) async-start(f32[32,128,128]{2,0,1:T(8,128)} %copy_bitcast_fusion), calls=%async_computation | async-start | bytes 4194304 | tf_op jit(solution)/shard_map/all_to_all | solution.py:98
  55.5 54.7 %all-to-all-start.1 = ((f32[32,128,128]{2,0,1:T(8,128)}), f32[32,128,128]{2,0,1:T(8,128)}, u32[]{:S(2)}, u32[]{:S(2)}) async-start(f32[32,128,128]{2,0,1:T(8,128)} %copy.32), calls=%async_computation.1 | async-start | bytes 4194304 | tf_op jit(solution)/shard_map/all_to_all | solution.py:109
where the time goes:
time: 201 us; the launch traced here: 200 us
  blocking collectives  67.6 us (34%)
  other arithmetic  35.6 us (18%)
  waiting for transfers between devices  25 us (12%)
  between operations  20.7 us (10%)
  matrix products  18.7 us (9%)
  starting transfers between devices  17.4 us (9%)
  local copies, waits for them, and re-layouts  15.1 us (8%)
    psum x1, blocking collectives, local(): gram_matrix = lax.psum(local_gram, ('hi', 'lo'))  67.6 us
    all_to_all x1, waiting for transfers between devices, local(): lax.all_to_all(shaped, ('hi', 'lo'), split_axis=1, concat_axis=1, tiled=T...  25 us
    add x1, other arithmetic, local(): diagonal = diagonal + fields[site_number] * spin_value(site_number)  17.3 us
    all_to_all x1, starting transfers between devices, local(): lax.all_to_all(shaped, ('hi', 'lo'), split_axis=1, concat_axis=1, tiled=T...  11.5 us
    sub x1, other arithmetic, local(): filtered = 4.0 / site_count * (applied + remote_part) - previous  9.63 us
    all_to_all x1, starting transfers between devices, local(): lax.all_to_all(bond_terms.reshape(arrived.shape), ('hi', 'lo'), split_axi...  5.89 us
  transfers between devices with their start and end apart: 2, of which 1 were waited for; matrix products, arithmetic and copies ran while one was open for 17% of the time, Pallas kernels for 0%

commit v1 on v0

--- a/solution.py
+++ b/solution.py
@@ -95,7 +95,12 @@
         ],
     )
     shaped = current.reshape(vectors, devices, amp_count // devices)
-    arrived = lax.all_to_all(shaped, ("hi", "lo"), split_axis=1, concat_axis=1, tiled=True)
+    arrived = jnp.concatenate(
+        lax.all_to_all(
+            jnp.stack(jnp.split(shaped, lax.axis_size(("hi", "lo")), axis=1)), ("hi", "lo"), 0, 0
+        ),
+        axis=1,
+    )
     count = arrived.shape[0]
     bond_terms = jnp.einsum(
         "vtl,tu->vul", arrived, far_matrix, precision=lax.Precision.HIGHEST

time: 201 us -> 281 us (1.40)
  local copies, waits for them, and re-layouts: 15.1 us -> 94.2 us
    unnamed x6 -> x133, local copies, waits for them, and re-layouts: 2.65 us -> 79.7 us
    reshape x1 -> x0, local copies, waits for them, and re-layouts: 3.2 us -> none  [local(): blocks = current.reshape(vectors, top_width, low_width)]
  transfers between devices with their start and end apart: 2 -> 2, of which waited for: 1 -> 1; matrix products, arithmetic and copies ran while one was open for 17% -> 11% of each run, Pallas kernels for 0% -> 0%
where the time goes in v1:
time: 281 us; the launch traced here: 280 us
  local copies, waits for them, and re-layouts  94.2 us (34%)
  blocking collectives  67.7 us (24%)
  other arithmetic  35.5 us (13%)
  waiting for transfers between devices  24.6 us (9%)
  between operations  21.1 us (8%)
  matrix products  19 us (7%)
  starting transfers between devices  17.8 us (6%)
    unnamed x133, local copies, waits for them, and re-layouts  79.7 us
    psum x1, blocking collectives, local(): gram_matrix = lax.psum(local_gram, ('hi', 'lo'))  67.7 us
    all_to_all x1, waiting for transfers between devices, local(): lax.all_to_all(jnp.stack(jnp.split(shaped, lax.axis_size(('hi', 'lo')), a...  24.6 us
    add x1, other arithmetic, local(): diagonal = diagonal + fields[site_number] * spin_value(site_number)  17.2 us
    all_to_all x1, starting transfers between devices, local(): lax.all_to_all(jnp.stack(jnp.split(shaped, lax.axis_size(('hi', 'lo')), a...  12 us
    sub x1, other arithmetic, local(): filtered = 4.0 / site_count * (applied + remote_part) - previous  9.63 us
    all_to_all x1, starting transfers between devices, local(): lax.all_to_all(bond_terms.reshape(arrived.shape), ('hi', 'lo'), split_axi...  5.88 us
  transfers between devices with their start and end apart: 2, of which 1 were waited for; matrix products, arithmetic and copies ran while one was open for 11% of the time, Pallas kernels for 0%

profile of v1, /device:TPU:1, one launch (start us, length us, event | category | flops | bytes accessed | tf_op | source)
XLA Modules:
  0.0 279.9 jit_solution(17634363238557099822)
XLA Ops:
  0.6 2.0 copy.541
  4.5 0.6 constant_dynamic-update-slice_fusion.127
  5.2 0.6 constant_dynamic-update-slice_fusion.126
  5.8 0.6 constant_dynamic-update-slice_fusion.125
  6.4 0.6 constant_dynamic-update-slice_fusion.124
  7.0 0.6 constant_dynamic-update-slice_fusion.123
  7.6 0.6 constant_dynamic-update-slice_fusion.122
  8.2 0.6 constant_dynamic-update-slice_fusion.121
  10.0 0.6 constant_dynamic-update-slice_fusion.118
  10.6 0.6 constant_dynamic-update-slice_fusion.117
  11.2 0.6 constant_dynamic-update-slice_fusion.116
  11.8 0.6 constant_dynamic-update-slice_fusion.115
  12.4 0.6 constant_dynamic-update-slice_fusion.114
  13.0 0.6 constant_dynamic-update-slice_fusion.113
  13.6 0.6 constant_dynamic-update-slice_fusion.112
  15.5 0.6 constant_dynamic-update-slice_fusion.109
  16.1 0.6 constant_dynamic-update-slice_fusion.108
  16.7 0.6 constant_dynamic-update-slice_fusion.107
  17.3 0.6 constant_dynamic-update-slice_fusion.106
  17.9 0.6 constant_dynamic-update-slice_fusion.105
  18.5 0.6 constant_dynamic-update-slice_fusion.104
  19.1 0.6 constant_dynamic-update-slice_fusion.103
  19.7 0.6 constant_dynamic-update-slice_fusion.102
  21.5 0.6 constant_dynamic-update-slice_fusion.99
  22.1 0.6 constant_dynamic-update-slice_fusion.98
  22.7 0.6 constant_dynamic-update-slice_fusion.97
  23.4 0.6 constant_dynamic-update-slice_fusion.96
  24.0 0.6 constant_dynamic-update-slice_fusion.95
  24.6 0.6 constant_dynamic-update-slice_fusion.94
  25.2 0.6 constant_dynamic-update-slice_fusion.93
  27.0 0.6 constant_dynamic-update-slice_fusion.90
  27.6 0.6 constant_dynamic-update-slice_fusion.89
  28.2 0.6 constant_dynamic-update-slice_fusion.88
  28.8 0.6 constant_dynamic-update-slice_fusion.87
  29.4 0.6 constant_dynamic-update-slice_fusion.86
  30.0 0.6 constant_dynamic-update-slice_fusion.85
  30.6 0.6 constant_dynamic-update-slice_fusion.84
  31.2 0.6 constant_dynamic-update-slice_fusion.83
  33.1 0.6 constant_dynamic-update-slice_fusion.80
  82.2 12.0 %all-to-all-start = ((f32[128,32,1,128]{3,1,2,0:T(8,128)}), f32[128,32,1,128]{3,1,2,0:T(8,128)}, u32[]{:S(2)}, u32[]{:S(2)}) async-start(f32[128,32,1,128]{3,1,2,0:T(8,128)} %constant_dynamic-update-slice_fusion), calls=%async_computation | async-start | bytes 4194304 | tf_op jit(solution)/shard_map/all_to_all | solution.py:99
  94.2 0.7 fusion.159
  99.3 24.6 %all-to-all-done = f32[128,32,1,128]{3,1,2,0:T(8,128)} async-done(((f32[128,32,1,128]{3,1,2,0:T(8,128)}), f32[128,32,1,128]{3,1,2,0:T(8,128)}, u32[]{:S(2)}, u32[]{:S(2)}) %all-to-all-start) | async-done | bytes 2097184 | tf_op jit(solution)/shard_map/all_to_all | solution.py:99
  123.9 2.8 %copy.402 = f32[128,32,1,128]{3,0,1,2:T(8,128)S(1)} copy(f32[128,32,1,128]{3,1,2,0:T(8,128)} %all-to-all-done) | data formatting | bytes 4194304 | tf_op jit(solution)/shard_map/all_to_all | solution.py:99
  126.7 1.1 fusion.5
  128.2 1.7 copy.404
  129.9 4.7 %bitcast_add_fusion.3 = f32[32,128,128]{2,1,0:T(8,128)S(1)} fusion(f32[32,128,128]{2,1,0:T(8,128)S(1)} %bitcast.523, f32[]{:T(128)S(6)} %mul.670, f32[]{:T(128)S(6)} %mul.669, f32[]{:T(128)S(6)} %mul.668, f32[]{:T(128)S(6)} %mul.667, f32[]{:T(128)S(6)} %mul.666, f32[]{:T(128)S(6)} %mul.665, s32[128]{0:T(128)S(1)} %get-tuple-element.190, ...), kind=kOutput, calls=%fused_computation.8 | convolution fusion | flops 806207488 | bytes 6295320 | tf_op jit(solution)/shard_map/vtl,tu->vul/dot_general | solution.py:105
  134.6 2.5 copy.405
  137.1 5.9 %all-to-all-start.1 = ((f32[32,128,128]{2,0,1:T(8,128)}), f32[32,128,128]{2,0,1:T(8,128)}, u32[]{:S(2)}, u32[]{:S(2)}) async-start(f32[32,128,128]{2,0,1:T(8,128)} %copy.405), calls=%async_computation.1 | async-start | bytes 4194304 | tf_op jit(solution)/shard_map/all_to_all | solution.py:114
  143.0 0.7 fusion.157
  155.7 3.4 %convolution_bitcast_fusion.1 = f32[32,128,128]{1,2,0:T(8,128)} fusion(f32[32,128,128]{2,1,0:T(8,128)S(1)} %bitcast.515, f32[]{:T(128)S(6)} %mul.659, f32[]{:T(128)S(6)} %mul.658, f32[]{:T(128)S(6)} %mul.657, f32[]{:T(128)S(6)} %mul.656, f32[]{:T(128)S(6)} %mul.655, f32[]{:T(128)S(6)} %mul.654, s32[128]{0:T(128)S(1)} %get-tuple-element.190, ...), kind=kOutput, calls=%fused_computation.14 | convolution fusion | flops 805683200 | bytes 4198168 | tf_op jit(solution)/shard_map/vtl,lu->vtu/dot_general | solution.py:82
  159.1 2.9 %copy.274 = f32[32,128,128]{2,1,0:T(8,128)} copy(f32[32,128,128]{1,2,0:T(8,128)} %convolution_bitcast_fusion.1) | data formatting | bytes 4194304 | tf_op jit(solution)/shard_map/vtl,lu->vtu/dot_general | solution.py:82
  166.6 17.2 %add_add_fusion = f32[16384]{0:T(1024)S(1)} fusion(f32[]{:T(128)S(6)} %mul.645, f32[]{:T(128)S(6)} %mul.644, f32[]{:T(128)S(6)} %mul.642, f32[]{:T(128)S(6)} %mul.641, f32[]{:T(128)S(6)} %mul.639, f32[]{:T(128)S(6)} %mul.638, f32[]{:T(128)S(6)} %mul.636, f32[]{:T(128)S(6)} %mul.635, f32[]{:T(128)S(6)} %mul.633, f32[]{:T(128)S(6)} %mul.632, f32[]{:T(128)S(6)} %mul.630, ...), kind=kLoop, calls=%fused_computation.189 | loop fusion | flops 2260992 | bytes 65704 | tf_op jit(solution)/shard_map/add | solution.py:59
  183.8 1.1 convolution_bitcast_fusion
  185.0 1.6 multiply_multiply_fusion.1
  186.5 3.4 %fusion.11 = f32[128,32,128]{2,0,1:T(8,128)} fusion(f32[32,128,128]{2,1,0:T(8,128)S(1)} %bitcast.517, f32[]{:T(128)S(6)} %mul.653, s32[128]{0:T(128)S(1)} %get-tuple-element.190, f32[]{:T(128)S(6)} %mul.652, s32[128]{0:T(128)S(1)} %get-tuple-element.191, f32[]{:T(128)S(6)} %mul.651, s32[128]{0:T(128)S(1)} %get-tuple-element.192, f32[]{:T(128)S(6)} %mul.650, ...), kind=kOutput, calls=%fused_computation.146 | convolution fusion | flops 805683200 | bytes 4198168 | tf_op jit(solution)/shard_map/vtl,tu->vul/dot_general | solution.py:79
  189.9 9.6 %fusion.2 = f32[32,16384]{1,0:T(8,128)S(1)} fusion(f32[32,16384]{1,0:T(8,128)} %param.4, f32[4,8,128,128]{3,2,1,0:T(8,128)} %bitcast.518, f32[4,8,128,128]{3,2,1,0:T(8,128)} %bitcast.521, f32[4,8,128,128]{3,2,1,0:T(8,128)} %bitcast.519, f32[32,16384]{1,0:T(8,128)} %param.5, f32[16384]{0:T(1024)S(1)} %add_add_fusion, f32[32,128,128]{2,0,1:T(8,128)} %all-to-all-done.1), kind=kLoop, calls=%fused_computation.3 | loop fusion | flops 3670016 | bytes 14745600 | tf_op jit(solution)/shard_map/sub | solution.py:117
  199.6 1.8 convolution_multiply_fusion
  201.3 67.7 %psum.7 = f32[32,32]{0,1:T(8,128)S(1)} all-reduce(f32[32,32]{0,1:T(8,128)S(1)} %convolution_multiply_fusion), channel_id=1, replica_groups=mesh['hi'=16,'lo'=8] {'hi','lo'}, use_global_device_ids=true, to_apply=%region_0.1 | all-reduce | flops 1024 | bytes 8192 | tf_op jit(solution)/shard_map/psum | solution.py:121
  269.1 2.9 %cholesky.17 = f32[32,32]{1,0:T(8,128)S(1)} custom-call(f32[32,32]{1,0:T(8,128)S(1)} %fusion.135), custom_call_target="Cholesky" | custom-call | tf_op jit(solution)/shard_map/jit(cholesky)/cholesky | solution.py:122
  272.0 0.6 compare_reduce_fusion
  272.7 0.7 fusion.136
  273.3 2.4 custom-call.7
  276.0 3.2 %fusion.160 = f32[32,16384]{1,0:T(8,128)} fusion(f32[32,32]{1,0:T(8,128)S(1)} %fusion.133, f32[32,16384]{1,0:T(8,128)S(1)} %fusion.2), kind=kOutput, calls=%fused_computation.310 | convolution fusion | flops 201326592 | bytes 4198400 | tf_op jit(solution)/shard_map/dot_general | solution.py:126
  279.2 0.7 copy.409
  (122 shorter events, 57.8 us)
Async XLA Ops:
  82.2 12.0 %copy-start = (s32[20]{0:T(128)S(1)}, s32[20]{0:T(128)}, u32[]{:S(2)}) copy-start(s32[20]{0:T(128)} %param.7) | copy-start | bytes 244
  82.2 17.1 %copy-start.1 = (s32[21]{0:T(128)S(1)}, s32[21]{0:T(128)}, u32[]{:S(2)}) copy-start(s32[21]{0:T(128)} %param.6) | copy-start | bytes 256
  82.2 41.7 %all-to-all-start = ((f32[128,32,1,128]{3,1,2,0:T(8,128)}), f32[128,32,1,128]{3,1,2,0:T(8,128)}, u32[]{:S(2)}, u32[]{:S(2)}) async-start(f32[128,32,1,128]{3,1,2,0:T(8,128)} %constant_dynamic-update-slice_fusion), calls=%async_computation | async-start | bytes 4194304 | tf_op jit(solution)/shard_map/all_to_all | solution.py:99
  137.1 52.8 %all-to-all-start.1 = ((f32[32,128,128]{2,0,1:T(8,128)}), f32[32,128,128]{2,0,1:T(8,128)}, u32[]{:S(2)}, u32[]{:S(2)}) async-start(f32[32,128,128]{2,0,1:T(8,128)} %copy.405), calls=%async_computation.1 | async-start | bytes 4194304 | tf_op jit(solution)/shard_map/all_to_all | solution.py:114
